TPU v7x, 32 devices: a whole 2x2x4 slice. The times are simulated.
32 devices in a mesh: shard: 4 (over x, core), replica: 8 (over z, y).
Axes of the slice: x: 2, y: 2, z: 4, core: 2. Of those that a mesh axis runs over, the one named last changes fastest.
Arguments:
- layer_input: bfloat16 [8192, 1600], P(('shard', 'replica')), may hold values from -6 to 6
- norm1_gain: bfloat16 [1600], P('shard'), may hold values from 0.5 to 1.5
- norm1_shift: bfloat16 [1600], P('shard'), may hold values from -3 to 3
- qkv_weight: bfloat16 [1600, 4800], P('shard')
- query_bias: bfloat16 [1600], P('shard'), may hold values from -3 to 3
- value_bias: bfloat16 [1600], P('shard'), may hold values from -3 to 3
- out_weight: bfloat16 [1600, 1600], P('shard'), may hold values from -0.625 to 0.625
- out_bias: bfloat16 [1600], P('shard'), may hold values from -3 to 3
- norm2_gain: bfloat16 [1600], P('shard'), may hold values from 0.5 to 1.5
- norm2_shift: bfloat16 [1600], P('shard'), may hold values from -3 to 3
- fc_weight: bfloat16 [1600, 6400], P('shard'), may hold values from -0.15625 to 0.15625
- fc_bias: bfloat16 [6400], P('shard'), may hold values from -3 to 3
- proj_weight: bfloat16 [6400, 1600], P('shard'), may hold values from -0.078125 to 0.078125
- proj_bias: bfloat16 [1600], P('shard'), may hold values from -3 to 3
- cotangent: bfloat16 [8192, 1600], P(('shard', 'replica')), may hold values from -6 to 6
- seq_lengths: int32 [128], replicated, may hold values from 0 to 256, as said below
- seq_device: int32 [128], replicated, may hold values from 0 to 31, as said below
- seq_offset: int32 [128], replicated, may hold values from 0 to 256, as said below
Outputs:
- output: bfloat16 [8192, 1600], P(('shard', 'replica'))
- grad_x: bfloat16 [8192, 1600], P(('shard', 'replica'))
- grad_norm1_gain: float32 [1600], P('shard')
- grad_norm1_shift: float32 [1600], P('shard')
- grad_qkv_weight: float32 [1600, 4800], P('shard')
- grad_query_bias: float32 [1600], P('shard')
- grad_value_bias: float32 [1600], P('shard')
- grad_out_weight: float32 [1600, 1600], P('shard')
- grad_out_bias: float32 [1600], P('shard')
- grad_norm2_gain: float32 [1600], P('shard')
- grad_norm2_shift: float32 [1600], P('shard')
- grad_fc_weight: float32 [1600, 6400], P('shard')
- grad_fc_bias: float32 [6400], P('shard')
- grad_proj_weight: float32 [6400, 1600], P('shard')
- grad_proj_bias: float32 [1600], P('shard')
Inputs may be any that keep to these rules, and one draw needn't show every extreme that they name: `seq_lengths`: some sequence has exactly 256 tokens; empty sequences occur. `seq_device`: device number = shard index * 8 + replica index; every device is named by exactly 4 sequences. The sequences of one device occupy disjoint ranges [seq_offset, seq_offset + seq_lengths) of its 256 positions.
All inputs are finite; a program needn't handle non-finite values.
Results may differ from a plain program's by a relative error of at most 0.018.
Values may be sent and summed in bfloat16 or wider, within the bound.
No kernel may reach another device: no remote copies, remote signals or barrier semaphores. Data moves between devices by JAX's collectives and lax.ppermute only.
A program may use at most 448 MiB of HBM per device.

v0:
```python
import math
import jax
import jax.numpy as jnp
from jax import lax
from jax.sharding import PartitionSpec as P

HEAD = 64
GELU_C = math.sqrt(2.0 / math.pi)


def normalize(values):
    centre = jnp.mean(values, axis=-1, keepdims=True)
    shifted = values - centre
    spread = jnp.mean(shifted * shifted, axis=-1, keepdims=True)
    inverse = lax.rsqrt(spread + 1e-05)
    return (shifted * inverse, inverse)


def norm_back(upstream, normed, inverse):
    first = jnp.mean(upstream, axis=-1, keepdims=True)
    second = jnp.mean(upstream * normed, axis=-1, keepdims=True)
    return inverse * (upstream - first - normed * second)


def gelu_pair(inputs):
    cubic = 0.044715 * inputs * inputs * inputs
    tangent = jnp.tanh(GELU_C * (inputs + cubic))
    value = 0.5 * inputs * (1.0 + tangent)
    slope = 0.5 * (1.0 + tangent) + 0.5 * inputs * (1.0 - tangent * tangent) * GELU_C * (
        1.0 + 3.0 * 0.044715 * inputs * inputs
    )
    return (value, slope)


def segment_ids(lengths, owners, offsets, device, count):
    position = jnp.arange(count, dtype=jnp.int32)
    number = jnp.arange(lengths.shape[0], dtype=jnp.int32)
    inside = (
        (owners[:, None] == device)
        & (position[None, :] >= offsets[:, None])
        & (position[None, :] < offsets[:, None] + lengths[:, None])
    )
    owned = jnp.sum(jnp.where(inside, number[:, None], 0), axis=0)
    filled = jnp.any(inside, axis=0)
    return (jnp.where(filled, owned, -1 - position), filled)


def product(spec, left, right):
    return jnp.einsum(spec, left, right, preferred_element_type=jnp.float32)


def mdot(left, right):
    return jnp.dot(left, right, preferred_element_type=jnp.float32)


def tdot(left, right):
    return lax.dot_general(
        left, right, (((0,), (0,)), ((), ())), preferred_element_type=jnp.float32
    )


def ndot(left, right):
    return lax.dot_general(
        left, right, (((1,), (1,)), ((), ())), preferred_element_type=jnp.float32
    )


def split_heads(packed, which):
    width_all = packed.shape[1] // 3
    return packed[:, which * width_all : (which + 1) * width_all].reshape(packed.shape[0], -1, HEAD)


def scores_of(packed, segment):
    raw = product("qhd,khd->hqk", split_heads(packed, 0), split_heads(packed, 1)) * (
        1.0 / math.sqrt(HEAD)
    )
    position = jnp.arange(packed.shape[0], dtype=jnp.int32)
    allowed = (segment[:, None] == segment[None, :]) & (position[None, :] <= position[:, None])
    return jnp.where(allowed[None], raw, -jnp.inf)


def forward(layer_input, segment, params):
    (
        gain1,
        shift1,
        w_qkv,
        b_query,
        b_value,
        w_out,
        b_out,
        gain2,
        shift2,
        w_fc,
        b_fc,
        w_proj,
        b_proj,
    ) = params
    count = layer_input.shape[0]
    inputs = layer_input.astype(jnp.float32)
    normed1, inverse1 = normalize(inputs)
    normed_in = (normed1 * gain1.astype(jnp.float32) + shift1.astype(jnp.float32)).astype(
        jnp.bfloat16
    )
    bias_all = jnp.concatenate(
        [
            b_query.astype(jnp.float32),
            jnp.zeros(b_query.shape, jnp.float32),
            b_value.astype(jnp.float32),
        ]
    )
    packed = (mdot(normed_in, w_qkv) + bias_all).astype(jnp.bfloat16)
    scores = scores_of(packed, segment)
    highest = jnp.max(scores, axis=-1, keepdims=True)
    expo = jnp.exp(scores - highest)
    total = jnp.sum(expo, axis=-1, keepdims=True)
    probs = (expo / total).astype(jnp.bfloat16)
    logsum = highest + jnp.log(total)
    mixed = (
        product("hqk,khd->qhd", probs, split_heads(packed, 2))
        .reshape(count, -1)
        .astype(jnp.bfloat16)
    )
    hidden = inputs + mdot(mixed, w_out) + b_out.astype(jnp.float32)
    normed2, inverse2 = normalize(hidden)
    mlp_in = (normed2 * gain2.astype(jnp.float32) + shift2.astype(jnp.float32)).astype(jnp.bfloat16)
    pre_act = mdot(mlp_in, w_fc) + b_fc.astype(jnp.float32)
    activ = gelu_pair(pre_act)[0].astype(jnp.bfloat16)
    result = (hidden + mdot(activ, w_proj) + b_proj.astype(jnp.float32)).astype(jnp.bfloat16)
    saved = (
        normed1,
        inverse1,
        normed_in,
        packed,
        mixed,
        logsum,
        segment,
        normed2,
        inverse2,
        mlp_in,
        pre_act,
        activ,
    )
    return (result, saved)


def attend_back(packed, grad_mixed, logsum, segment):
    count = packed.shape[0]
    scores = scores_of(packed, segment)
    back_probs = jnp.exp(scores - logsum)
    probs_low = back_probs.astype(jnp.bfloat16)
    upstream = grad_mixed.reshape(count, -1, HEAD)
    grad_values = product("hqk,qhd->khd", probs_low, upstream)
    grad_probs = product("qhd,khd->hqk", upstream, split_heads(packed, 2))
    delta = jnp.sum(back_probs * grad_probs, axis=-1, keepdims=True)
    grad_scores = (back_probs * (grad_probs - delta) * (1.0 / math.sqrt(HEAD))).astype(jnp.bfloat16)
    grad_query = product("hqk,khd->qhd", grad_scores, split_heads(packed, 1))
    grad_keys = product("hqk,qhd->khd", grad_scores, split_heads(packed, 0))
    return jnp.concatenate(
        [
            grad_query.reshape(count, -1),
            grad_keys.reshape(count, -1),
            grad_values.reshape(count, -1),
        ],
        axis=1,
    )


def backward(cotangent, filled, saved, params):
    (
        gain1,
        shift1,
        w_qkv,
        b_query,
        b_value,
        w_out,
        b_out,
        gain2,
        shift2,
        w_fc,
        b_fc,
        w_proj,
        b_proj,
    ) = params
    (
        normed1,
        inverse1,
        normed_in,
        packed,
        mixed,
        logsum,
        segment,
        normed2,
        inverse2,
        mlp_in,
        pre_act,
        activ,
    ) = saved
    upstream = jnp.where(filled[:, None], cotangent.astype(jnp.float32), 0.0)
    upstream_low = upstream.astype(jnp.bfloat16)
    grad_bproj = jnp.sum(upstream, axis=0)
    slope = gelu_pair(pre_act)[1]
    grad_pre = ndot(upstream_low, w_proj) * slope
    grad_pre_low = grad_pre.astype(jnp.bfloat16)
    grad_bfc = jnp.sum(grad_pre, axis=0)
    grad_mlp_in = ndot(grad_pre_low, w_fc)
    grad_gain2 = jnp.sum(grad_mlp_in * normed2, axis=0)
    grad_shift2 = jnp.sum(grad_mlp_in, axis=0)
    grad_hidden = upstream + norm_back(grad_mlp_in * gain2.astype(jnp.float32), normed2, inverse2)
    grad_bout = jnp.sum(grad_hidden, axis=0)
    grad_hidden_low = grad_hidden.astype(jnp.bfloat16)
    grad_mixed = ndot(grad_hidden_low, w_out).astype(jnp.bfloat16)
    grad_packed = attend_back(packed, grad_mixed, logsum, segment)
    width_all = w_out.shape[0]
    grad_bquery = jnp.sum(grad_packed[:, :width_all], axis=0)
    grad_bvalue = jnp.sum(grad_packed[:, 2 * width_all :], axis=0)
    grad_packed_low = grad_packed.astype(jnp.bfloat16)
    grad_in = ndot(grad_packed_low, w_qkv)
    grad_gain1 = jnp.sum(grad_in * normed1, axis=0)
    grad_shift1 = jnp.sum(grad_in, axis=0)
    grad_inputs = (
        grad_hidden + norm_back(grad_in * gain1.astype(jnp.float32), normed1, inverse1)
    ).astype(jnp.bfloat16)
    grad_wqkv = tdot(normed_in, grad_packed_low)
    grad_wout = tdot(mixed, grad_hidden_low)
    grad_wfc = tdot(mlp_in, grad_pre_low)
    grad_wproj = tdot(activ, upstream_low)
    grads = (
        grad_gain1,
        grad_shift1,
        grad_wqkv,
        grad_bquery,
        grad_bvalue,
        grad_wout,
        grad_bout,
        grad_gain2,
        grad_shift2,
        grad_wfc,
        grad_bfc,
        grad_wproj,
        grad_bproj,
    )
    lefts = (normed_in, mixed, mlp_in, activ)
    rights = (grad_packed_low, grad_hidden_low, grad_pre_low, upstream_low)
    return (grad_inputs, grads, lefts, rights)


def local(
    layer_input,
    norm1_gain,
    norm1_shift,
    qkv_weight,
    query_bias,
    value_bias,
    out_weight,
    out_bias,
    norm2_gain,
    norm2_shift,
    fc_weight,
    fc_bias,
    proj_weight,
    proj_bias,
    cotangent,
    seq_lengths,
    seq_device,
    seq_offset,
):
    gathered = (
        lax.all_gather(norm1_gain, "shard", axis=0, tiled=True),
        lax.all_gather(norm1_shift, "shard", axis=0, tiled=True),
        lax.all_gather(qkv_weight, "shard", axis=0, tiled=True),
        lax.all_gather(query_bias, "shard", axis=0, tiled=True),
        lax.all_gather(value_bias, "shard", axis=0, tiled=True),
        lax.all_gather(out_weight, "shard", axis=0, tiled=True),
        lax.all_gather(out_bias, "shard", axis=0, tiled=True),
        lax.all_gather(norm2_gain, "shard", axis=0, tiled=True),
        lax.all_gather(norm2_shift, "shard", axis=0, tiled=True),
        lax.all_gather(fc_weight, "shard", axis=0, tiled=True),
        lax.all_gather(fc_bias, "shard", axis=0, tiled=True),
        lax.all_gather(proj_weight, "shard", axis=0, tiled=True),
        lax.all_gather(proj_bias, "shard", axis=0, tiled=True),
    )
    device = lax.axis_index("shard") * lax.axis_size("replica") + lax.axis_index("replica")
    segment, filled = segment_ids(seq_lengths, seq_device, seq_offset, device, layer_input.shape[0])
    result, saved = forward(layer_input, segment, gathered)
    gathered = (
        lax.all_gather(norm1_gain, "shard", axis=0, tiled=True),
        lax.all_gather(norm1_shift, "shard", axis=0, tiled=True),
        lax.all_gather(qkv_weight, "shard", axis=0, tiled=True),
        lax.all_gather(query_bias, "shard", axis=0, tiled=True),
        lax.all_gather(value_bias, "shard", axis=0, tiled=True),
        lax.all_gather(out_weight, "shard", axis=0, tiled=True),
        lax.all_gather(out_bias, "shard", axis=0, tiled=True),
        lax.all_gather(norm2_gain, "shard", axis=0, tiled=True),
        lax.all_gather(norm2_shift, "shard", axis=0, tiled=True),
        lax.all_gather(fc_weight, "shard", axis=0, tiled=True),
        lax.all_gather(fc_bias, "shard", axis=0, tiled=True),
        lax.all_gather(proj_weight, "shard", axis=0, tiled=True),
        lax.all_gather(proj_bias, "shard", axis=0, tiled=True),
    )
    grad_inputs, grads, lefts, rights = backward(cotangent, filled, saved, gathered)
    parts = (
        lax.psum_scatter(
            grads[0].astype(jnp.bfloat16), "shard", scatter_dimension=0, tiled=True
        ).astype(jnp.float32),
        lax.psum_scatter(
            grads[1].astype(jnp.bfloat16), "shard", scatter_dimension=0, tiled=True
        ).astype(jnp.float32),
        lax.psum_scatter(
            grads[2].astype(jnp.bfloat16), "shard", scatter_dimension=0, tiled=True
        ).astype(jnp.float32),
        lax.psum_scatter(
            grads[3].astype(jnp.bfloat16), "shard", scatter_dimension=0, tiled=True
        ).astype(jnp.float32),
        lax.psum_scatter(
            grads[4].astype(jnp.bfloat16), "shard", scatter_dimension=0, tiled=True
        ).astype(jnp.float32),
        lax.psum_scatter(
            grads[5].astype(jnp.bfloat16), "shard", scatter_dimension=0, tiled=True
        ).astype(jnp.float32),
        lax.psum_scatter(
            grads[6].astype(jnp.bfloat16), "shard", scatter_dimension=0, tiled=True
        ).astype(jnp.float32),
        lax.psum_scatter(
            grads[7].astype(jnp.bfloat16), "shard", scatter_dimension=0, tiled=True
        ).astype(jnp.float32),
        lax.psum_scatter(
            grads[8].astype(jnp.bfloat16), "shard", scatter_dimension=0, tiled=True
        ).astype(jnp.float32),
        lax.psum_scatter(
            grads[9].astype(jnp.bfloat16), "shard", scatter_dimension=0, tiled=True
        ).astype(jnp.float32),
        lax.psum_scatter(
            grads[10].astype(jnp.bfloat16), "shard", scatter_dimension=0, tiled=True
        ).astype(jnp.float32),
        lax.psum_scatter(
            grads[11].astype(jnp.bfloat16), "shard", scatter_dimension=0, tiled=True
        ).astype(jnp.float32),
        lax.psum_scatter(
            grads[12].astype(jnp.bfloat16), "shard", scatter_dimension=0, tiled=True
        ).astype(jnp.float32),
    )
    totals = (
        lax.psum(parts[0].astype(jnp.bfloat16), "replica").astype(jnp.float32),
        lax.psum(parts[1].astype(jnp.bfloat16), "replica").astype(jnp.float32),
        lax.psum(parts[2].astype(jnp.bfloat16), "replica").astype(jnp.float32),
        lax.psum(parts[3].astype(jnp.bfloat16), "replica").astype(jnp.float32),
        lax.psum(parts[4].astype(jnp.bfloat16), "replica").astype(jnp.float32),
        lax.psum(parts[5].astype(jnp.bfloat16), "replica").astype(jnp.float32),
        lax.psum(parts[6].astype(jnp.bfloat16), "replica").astype(jnp.float32),
        lax.psum(parts[7].astype(jnp.bfloat16), "replica").astype(jnp.float32),
        lax.psum(parts[8].astype(jnp.bfloat16), "replica").astype(jnp.float32),
        lax.psum(parts[9].astype(jnp.bfloat16), "replica").astype(jnp.float32),
        lax.psum(parts[10].astype(jnp.bfloat16), "replica").astype(jnp.float32),
        lax.psum(parts[11].astype(jnp.bfloat16), "replica").astype(jnp.float32),
        lax.psum(parts[12].astype(jnp.bfloat16), "replica").astype(jnp.float32),
    )
    return (
        result,
        grad_inputs,
        totals[0],
        totals[1],
        totals[2],
        totals[3],
        totals[4],
        totals[5],
        totals[6],
        totals[7],
        totals[8],
        totals[9],
        totals[10],
        totals[11],
        totals[12],
    )


def solution(mesh):
    placed = (
        P(("shard", "replica"), None),
        P("shard"),
        P("shard"),
        P("shard", None),
        P("shard"),
        P("shard"),
        P("shard", None),
        P("shard"),
        P("shard"),
        P("shard"),
        P("shard", None),
        P("shard"),
        P("shard", None),
        P("shard"),
        P(("shard", "replica"), None),
        P(),
        P(),
        P(),
    )
    return jax.shard_map(
        local,
        mesh=mesh,
        in_specs=placed,
        out_specs=(
            P(("shard", "replica"), None),
            P(("shard", "replica"), None),
            P("shard"),
            P("shard"),
            P("shard", None),
            P("shard"),
            P("shard"),
            P("shard", None),
            P("shard"),
            P("shard"),
            P("shard"),
            P("shard", None),
            P("shard"),
            P("shard", None),
            P("shard"),
        ),
        check_vma=False,
    )
```

profile of v0, /device:TPU:0, one launch (start us, length us, event | category | flops | bytes accessed | tf_op | source)
XLA Modules:
  0.0 1449.5 jit_solution(5690311170459568473)
XLA Ops:
  7.2 0.7 all-gather.5.cloned.1.call-update
  8.0 0.7 all-gather.7.cloned.1.call-update
  8.8 0.7 all-gather.9.cloned.1.call-update
  9.6 0.5 all-gather.11.cloned.1.call-update
  10.2 0.6 fusion.76
  12.1 0.3 dynamic-update-slice.5
  12.3 0.2 dynamic-update-slice.6
  13.4 0.2 dynamic-update-slice.3
  13.9 0.3 dynamic-update-slice.7
  14.2 14.2 all-reduce.21
  29.1 0.3 fusion.45
  29.5 82.0 %all-gather.5.cloned.1.call-done = bf16[1600,4800]{1,0:T(8,128)(2,1)} async-done(((bf16[400,4800]{1,0:T(8,128)(2,1)}), bf16[1600,4800]{1,0:T(8,128)(2,1)}) %all-gather.5.cloned.1.call-update) | async-done | bytes 15360016 | tf_op jit(solution)/shard_map/all_gather | solution.py:270
  111.5 14.2 fusion.7
  125.7 1.8 fusion.75
  127.5 0.9 copy-done.4
  128.4 1.2 fusion.77
  129.7 1.1 fusion.8
  130.8 1.6 copy-done
  132.4 1.7 fusion.51
  134.2 19.9 %all-gather.7.cloned.1.call-done = bf16[1600,1600]{1,0:T(8,128)(2,1)} async-done(((bf16[400,1600]{1,0:T(8,128)(2,1)}), bf16[1600,1600]{1,0:T(8,128)(2,1)}) %all-gather.7.cloned.1.call-update) | async-done | bytes 5120016 | tf_op jit(solution)/shard_map/all_gather | solution.py:273
  154.0 4.9 fusion.78
  159.0 0.2 multiply_reduce_fusion.3
  159.2 125.3 %all-gather.9.cloned.1.call-done = bf16[1600,6400]{1,0:T(8,128)(2,1)} async-done(((bf16[400,6400]{1,0:T(8,128)(2,1)}), bf16[1600,6400]{1,0:T(8,128)(2,1)}) %all-gather.9.cloned.1.call-update) | async-done | bytes 20480016 | tf_op jit(solution)/shard_map/all_gather | solution.py:277
  284.5 12.7 convolution_add_fusion
  297.2 122.2 %all-gather.11.cloned.1.call-done = bf16[6400,1600]{1,0:T(8,128)(2,1)} async-done(((bf16[1600,1600]{1,0:T(8,128)(2,1)}), bf16[6400,1600]{1,0:T(8,128)(2,1)}) %all-gather.11.cloned.1.call-update) | async-done | bytes 20480016 | tf_op jit(solution)/shard_map/all_gather | solution.py:279
  419.4 13.5 fusion.81
  432.9 13.1 multiply_reduce_fusion.1
  446.1 1.0 fusion.74
  447.2 4.0 convolution_convert_fusion.3
  451.5 4.2 convolution_convert_fusion.4
  455.8 0.9 copy-done.8
  456.6 4.6 fusion.82
  461.2 12.9 fusion.52
  474.1 13.4 bitcast_convert_fusion.1
  487.6 5.8 bitcast_convert_fusion
  493.4 12.1 convolution_convert_fusion.2
  505.6 16.7 %convolution_convert_fusion = bf16[6400,1600]{1,0:T(8,128)(2,1)} fusion(bf16[256,1600]{0,1:T(8,128)(2,1)} %param.32, pred[256]{0:T(512)(128)(4,1)S(1)} %fusion.63, f32[256,6400]{1,0:T(8,128)} %convolution_add_fusion), kind=kOutput, calls=%fused_computation.1 | convolution fusion | flops 5269094400 | bytes 27853056 | tf_op jit(solution)/shard_map/dot_general | solution.py:57
  522.3 12.6 convolution_convert_fusion.1
  535.0 90.8 %reduce-scatter.5.cloned.1.call-done = bf16[400,4800]{1,0:T(8,128)(2,1)} async-done(((bf16[1600,4800]{1,0:T(8,128)(2,1)}), bf16[400,4800]{1,0:T(8,128)(2,1)}) %reduce-scatter.5.cloned.1.call-update) | async-done | bytes 3840016 | tf_op jit(solution)/shard_map/reduce_scatter | solution.py:308
  625.8 155.1 %reduce-scatter.11.cloned.1.call-done = bf16[1600,1600]{1,0:T(8,128)(2,1)} async-done(((bf16[6400,1600]{1,0:T(8,128)(2,1)}), bf16[1600,1600]{1,0:T(8,128)(2,1)}) %reduce-scatter.11.cloned.1.call-update) | async-done | bytes 5120016 | tf_op jit(solution)/shard_map/reduce_scatter | solution.py:335
  781.0 158.1 %reduce-scatter.9.cloned.1.call-done = bf16[400,6400]{1,0:T(8,128)(2,1)} async-done(((bf16[1600,6400]{1,0:T(8,128)(2,1)}), bf16[400,6400]{1,0:T(8,128)(2,1)}) %reduce-scatter.9.cloned.1.call-update) | async-done | bytes 5120016 | tf_op jit(solution)/shard_map/reduce_scatter | solution.py:329
  940.4 0.3 dynamic-update-slice.8
  940.7 1.7 bitcast_reduce_fusion
  942.5 1.7 bitcast_reduce_fusion.1
  944.3 13.3 fusion.44
  957.6 11.5 all-reduce.20
  969.8 39.6 %all-reduce.18 = (bf16[400]{0:T(512)(128)(2,1)S(1)}, bf16[400]{0:T(512)(128)(2,1)S(1)}, bf16[400]{0:T(512)(128)(2,1)S(1)}, bf16[400]{0:T(512)(128)(2,1)S(1)}, bf...) all-reduce(bf16[400]{0:T(512)(128)(2,1)S(1)} %dynamic-slice.10, ...), channel_id=1, replica_groups=mesh['shard'=4,'replica'=8] {'replica'}, use_global_device_ids=true, to_apply=%region_15.16 | all-reduce | flops 4800 | bytes 19200 | tf_op jit(solution)/shard_map/psum | solution.py:343
  1009.4 0.6 convert_element_type.222
  1010.0 0.6 convert_element_type.224
  1010.6 0.6 convert_element_type.229
  1011.1 0.6 convert_element_type.232
  1011.7 0.6 convert_element_type.236
  1012.3 0.6 convert_element_type.238
  1012.9 0.6 convert_element_type.240
  1013.5 0.6 convert_element_type.248
  1014.0 0.6 convert_element_type.244
  1014.7 3.1 fusion.43
  1017.8 17.3 %fusion.30 = bf16[256,1600]{0,1:T(8,128)(2,1)} fusion(f32[256,1600]{0,1:T(8,128)S(1)} %get-tuple-element.65, bf16[6400,1600]{1,0:T(8,128)(2,1)} %all-gather.11.cloned.1.call-done, f32[1600]{0:T(1024)S(1)} %convert_element_type.211, f32[256,6400]{1,0:T(8,128)} %convolution_add_fusion), kind=kOutput, calls=%fused_computation.39 | convolution fusion | flops 5258854400 | bytes 29497600 | tf_op jit(solution)/shard_map/dot_general | solution.py:53
  1035.1 389.8 %all-reduce.24.cloned.1.call-done = (bf16[400,4800]{1,0:T(8,128)(2,1)}, bf16[400,1600]{1,0:T(8,128)(2,1)}, bf16[400,6400]{1,0:T(8,128)(2,1)}, bf16[1600,1600]{1,0:T(8,128)(2,1)}) async-done(((bf16[400,4800]{1,0:T(8,128)(2,1)}, bf16[400,1600]{1,0:T(8,128)(2,1)}, bf16[400,6400]{1,0:T(8,128)(2,1)}, bf16[1600,1600]{1,0:T(8,128)(2,1)}), (bf16[400,4800]{1,0:T(8,128)(2,1)}, bf16[400,1600]{1,0:T(8,128)(2,1)}, ...) | async-done | bytes 15360016 | tf_op jit(solution)/shard_map/psum | solution.py:345
  1424.9 3.1 convert_element_type.234
  1428.0 4.5 convert_element_type.226
  1432.5 0.5 copy-done.2
  1433.0 4.7 convert_element_type.242
  1437.7 4.8 convert_element_type.246
  (116 shorter events, 3.5 us)
Async XLA Ops:
  7.2 104.3 %all-gather.5.cloned.1.call-start = ((), (), s32[]{:S(2)}) async-start(), calls=%async_computation.4 | async-start | bytes 19456000 | tf_op jit(solution)/shard_map/all_gather | solution.py:270
  7.9 146.1 %all-gather.7.cloned.1.call-start = ((), (), s32[]{:S(2)}) async-start(), calls=%async_computation.5 | async-start | bytes 6656000 | tf_op jit(solution)/shard_map/all_gather | solution.py:273
  8.7 1.5 copy-start.14
  8.7 3.4 copy-start.16
  8.7 3.7 copy-start.17
  8.7 3.9 copy-start.18
  8.7 4.1 copy-start.19
  8.7 4.4 copy-start.20
  8.7 4.6 copy-start.21
  8.7 4.9 copy-start.22
  8.8 5.1 copy-start.13
  8.8 19.7 %copy-start.15 = (s32[128]{0:T(128)S(1)}, s32[128]{0:T(128)}, u32[]{:S(2)}) copy-start(s32[128]{0:T(128)} %param.35) | copy-start | bytes 1540
  8.8 19.7 %copy-start.24 = (s32[128]{0:T(128)S(1)}, s32[128]{0:T(128)}, u32[]{:S(2)}) copy-start(s32[128]{0:T(128)} %param.33) | copy-start | bytes 1540
  8.8 19.8 %copy-start.25 = (s32[128]{0:T(128)S(1)}, s32[128]{0:T(128)}, u32[]{:S(2)}) copy-start(s32[128]{0:T(128)} %param.34) | copy-start | bytes 1540
  8.8 20.0 %copy-start.1 = (bf16[256,1600]{0,1:T(8,128)(2,1)S(1)}, bf16[256,1600]{0,1:T(8,128)(2,1)}, u32[]{:S(2)}) copy-start(bf16[256,1600]{0,1:T(8,128)(2,1)} %param.18) | copy-start | bytes 2457604
  8.8 275.7 %all-gather.9.cloned.1.call-start = ((), (), s32[]{:S(2)}) async-start(), calls=%async_computation.6 | async-start | bytes 25600000 | tf_op jit(solution)/shard_map/all_gather | solution.py:277
  9.5 409.8 %all-gather.11.cloned.1.call-start = ((), (), s32[]{:S(2)}) async-start(), calls=%async_computation.7 | async-start | bytes 26624000 | tf_op jit(solution)/shard_map/all_gather | solution.py:279
  10.1 524.9 %reduce-scatter.7.cloned.1.call-start = ((), (), s32[]{:S(2)}) async-start(), calls=%async_computation.9 | async-start | bytes 6656000 | tf_op jit(solution)/shard_map/reduce_scatter | solution.py:317
  127.5 0.9 copy-start.4
  127.5 2.2 copy-start.5
  127.5 3.3 copy-start.6
  129.6 2.8 copy-start
  134.2 24.8 %copy-start.9 = (bf16[25,64,256]{2,1,0:T(8,128)(2,1)}, bf16[25,64,256]{2,1,0:T(8,128)(2,1)S(1)}, u32[]{:S(2)}) copy-start(bf16[25,64,256]{2,1,0:T(8,128)(2,1)S(1)} %fusion.51) | copy-start | bytes 2457604
  159.2 260.2 %copy-start.11 = (bf16[256,1600]{0,1:T(8,128)(2,1)S(1)}, bf16[256,1600]{0,1:T(8,128)(2,1)}, u32[]{:S(2)}) copy-start(bf16[256,1600]{0,1:T(8,128)(2,1)} %param.32) | copy-start | bytes 2457604
  432.9 13.2 copy-start.12
  446.1 1.1 copy-start.10
  451.2 174.6 %reduce-scatter.5.cloned.1.call-start = ((), (), s32[]{:S(2)}) async-start(), calls=%async_computation.8 | async-start | bytes 19456000 | tf_op jit(solution)/shard_map/reduce_scatter | solution.py:308
  451.5 5.2 copy-start.7
  455.7 0.9 copy-start.8
  505.5 275.5 %reduce-scatter.11.cloned.1.call-start = ((), (), s32[]{:S(2)}) async-start(), calls=%async_computation.11 | async-start | bytes 26624000 | tf_op jit(solution)/shard_map/reduce_scatter | solution.py:335
  522.3 416.8 %reduce-scatter.9.cloned.1.call-start = ((), (), s32[]{:S(2)}) async-start(), calls=%async_computation.10 | async-start | bytes 25600000 | tf_op jit(solution)/shard_map/reduce_scatter | solution.py:329
  534.9 889.9 %all-reduce.24.cloned.1.call-start = ((), (), s32[]{:S(2)}) async-start(), calls=%async_computation.12 | async-start | bytes 31334400 | tf_op jit(solution)/shard_map/psum | solution.py:345
  939.1 1.3 copy-start.23
  1424.9 3.2 copy-start.3
  1428.0 4.9 copy-start.2
  1428.0 9.6 slice-start
  1433.0 4.7 slice-start.1
Sparse Core Ops, SparseCore 0:
  9.6 101.8 all-gather.4
  113.0 40.9 all-gather.6
  155.6 128.8 all-gather.8
  285.9 133.3 all-gather.10
  451.4 51.8 reduce-scatter.6
  505.8 119.9 reduce-scatter.4
  628.4 152.4 reduce-scatter.10
  783.6 155.4 reduce-scatter.8
  943.8 481.0 all-reduce.23
where the time goes:
time: 1450 us
  waiting for transfers between devices  1150 us (79%)
  matrix products  178 us (12%)
  blocking collectives  65.2 us (4%)
  other arithmetic  32.3 us (2%)
  between operations  17.4 us (1%)
    psum x1, waiting for transfers between devices, local(): lax.psum(parts[2].astype(jnp.bfloat16), 'replica').astype(jnp.float32)  390 us
    reduce_scatter x1, waiting for transfers between devices, local(): lax.psum_scatter(grads[9].astype(jnp.bfloat16), 'shard', scatter_dimensio...  158 us
    reduce_scatter x1, waiting for transfers between devices, local(): lax.psum_scatter(grads[11].astype(jnp.bfloat16), 'shard', scatter_dimensi...  155 us
    all_gather x1, waiting for transfers between devices, local(): lax.all_gather(fc_weight, 'shard', axis=0, tiled=True)  125 us
    all_gather x1, waiting for transfers between devices, local(): lax.all_gather(proj_weight, 'shard', axis=0, tiled=True)  122 us
    reduce_scatter x1, waiting for transfers between devices, local(): lax.psum_scatter(grads[2].astype(jnp.bfloat16), 'shard', scatter_dimensio...  90.8 us
    all_gather x1, waiting for transfers between devices, local(): lax.all_gather(qkv_weight, 'shard', axis=0, tiled=True)  82 us
    dot_general x4, matrix products, mdot(): return jnp.dot(left, right, preferred_element_type=jnp.float32)  49.2 us
  transfers between devices with their start and end apart: 9, of which 8 were waited for; matrix products, arithmetic and copies ran while one was open for 12% of the time, Pallas kernels for 0%

commit v1 on v0

--- a/solution.py
+++ b/solution.py
@@ -342,7 +342,9 @@
     totals = (
         lax.psum(parts[0].astype(jnp.bfloat16), "replica").astype(jnp.float32),
         lax.psum(parts[1].astype(jnp.bfloat16), "replica").astype(jnp.float32),
-        lax.psum(parts[2].astype(jnp.bfloat16), "replica").astype(jnp.float32),
+        jnp.sum(lax.all_gather(parts[2].astype(jnp.bfloat16), "replica"), axis=0).astype(
+            jnp.float32
+        ),
         lax.psum(parts[3].astype(jnp.bfloat16), "replica").astype(jnp.float32),
         lax.psum(parts[4].astype(jnp.bfloat16), "replica").astype(jnp.float32),
         lax.psum(parts[5].astype(jnp.bfloat16), "replica").astype(jnp.float32),

time: 1450 us -> 1930 us (1.33)
  waiting for transfers between devices: 1150 us -> 1600 us
    all_gather x0 -> x1, waiting for transfers between devices: none -> 577 us  [local(): lax.all_gather(parts[2].astype(jnp.bfloat16), 'replica')]
    psum x1, waiting for transfers between devices: 390 us -> 271 us  [local(): lax.psum(parts[5].astype(jnp.bfloat16), 'replica').astype(jnp.float32)]
    reduce_scatter x1, waiting for transfers between devices: 155 us -> 122 us  [local(): lax.psum_scatter(grads[11].astype(jnp.bfloat16), 'shard', scatter_dimensi...]
    reduce_scatter x1, waiting for transfers between devices: 90.8 us -> 122 us  [local(): lax.psum_scatter(grads[2].astype(jnp.bfloat16), 'shard', scatter_dimensio...]
  transfers between devices with their start and end apart: 9 -> 10, of which waited for: 8 -> 9; matrix products, arithmetic and copies ran while one was open for 12% -> 10% of each run, Pallas kernels for 0% -> 0%
where the time goes in v1:
time: 1930 us; the launch traced here: 1920 us
  waiting for transfers between devices  1600 us (83%)
  matrix products  180 us (9%)
  blocking collectives  65.2 us (3%)
  other arithmetic  50 us (3%)
    all_gather x1, waiting for transfers between devices, local(): lax.all_gather(parts[2].astype(jnp.bfloat16), 'replica')  577 us
    psum x1, waiting for transfers between devices, local(): lax.psum(parts[5].astype(jnp.bfloat16), 'replica').astype(jnp.float32)  271 us
    reduce_scatter x1, waiting for transfers between devices, local(): lax.psum_scatter(grads[9].astype(jnp.bfloat16), 'shard', scatter_dimensio...  158 us
    all_gather x1, waiting for transfers between devices, local(): lax.all_gather(fc_weight, 'shard', axis=0, tiled=True)  125 us
    reduce_scatter x1, waiting for transfers between devices, local(): lax.psum_scatter(grads[2].astype(jnp.bfloat16), 'shard', scatter_dimensio...  122 us
    reduce_scatter x1, waiting for transfers between devices, local(): lax.psum_scatter(grads[11].astype(jnp.bfloat16), 'shard', scatter_dimensi...  122 us
    all_gather x1, waiting for transfers between devices, local(): lax.all_gather(proj_weight, 'shard', axis=0, tiled=True)  122 us
    all_gather x1, waiting for transfers between devices, local(): lax.all_gather(qkv_weight, 'shard', axis=0, tiled=True)  81.9 us
  transfers between devices with their start and end apart: 10, of which 9 were waited for; matrix products, arithmetic and copies ran while one was open for 10% of the time, Pallas kernels for 0%

profile of v1, /device:TPU:0, one launch (start us, length us, event | category | flops | bytes accessed | tf_op | source)
XLA Modules:
  0.0 1924.9 jit_solution(8266711582846910500)
XLA Ops:
  7.2 0.7 all-gather.7.cloned.1.call-update
  8.0 0.7 all-gather.9.cloned.1.call-update
  8.8 0.7 all-gather.11.cloned.1.call-update
  9.6 0.5 all-gather.13.cloned.1.call-update
  10.2 0.6 fusion.76
  12.1 0.3 dynamic-update-slice.5
  13.9 0.3 dynamic-update-slice.7
  14.2 14.2 all-reduce.21
  29.2 0.3 fusion.45
  29.6 81.9 %all-gather.7.cloned.1.call-done = bf16[1600,4800]{1,0:T(8,128)(2,1)} async-done(((bf16[400,4800]{1,0:T(8,128)(2,1)}), bf16[1600,4800]{1,0:T(8,128)(2,1)}) %all-gather.7.cloned.1.call-update) | async-done | bytes 15360016 | tf_op jit(solution)/shard_map/all_gather | solution.py:270
  111.5 14.2 fusion.7
  125.7 1.8 fusion.75
  127.5 0.9 copy-done.2
  128.4 1.2 fusion.77
  129.7 1.1 fusion.8
  130.8 1.6 copy-done
  132.4 1.8 fusion.51
  134.2 19.8 %all-gather.9.cloned.1.call-done = bf16[1600,1600]{1,0:T(8,128)(2,1)} async-done(((bf16[400,1600]{1,0:T(8,128)(2,1)}), bf16[1600,1600]{1,0:T(8,128)(2,1)}) %all-gather.9.cloned.1.call-update) | async-done | bytes 5120016 | tf_op jit(solution)/shard_map/all_gather | solution.py:273
  154.0 4.9 fusion.78
  159.0 0.3 multiply_reduce_fusion.3
  159.2 125.3 %all-gather.11.cloned.1.call-done = bf16[1600,6400]{1,0:T(8,128)(2,1)} async-done(((bf16[400,6400]{1,0:T(8,128)(2,1)}), bf16[1600,6400]{1,0:T(8,128)(2,1)}) %all-gather.11.cloned.1.call-update) | async-done | bytes 20480016 | tf_op jit(solution)/shard_map/all_gather | solution.py:277
  284.5 12.7 convolution_add_fusion
  297.2 122.1 %all-gather.13.cloned.1.call-done = bf16[6400,1600]{1,0:T(8,128)(2,1)} async-done(((bf16[1600,1600]{1,0:T(8,128)(2,1)}), bf16[6400,1600]{1,0:T(8,128)(2,1)}) %all-gather.13.cloned.1.call-update) | async-done | bytes 20480016 | tf_op jit(solution)/shard_map/all_gather | solution.py:279
  419.4 13.5 fusion.81
  432.9 13.3 multiply_reduce_fusion.1
  446.2 1.0 fusion.74
  447.3 4.0 convolution_convert_fusion.3
  451.5 14.5 convolution_convert_fusion
  466.1 12.2 convolution_convert_fusion.1
  478.3 0.3 reduce-scatter.5.cloned.1.call-start
  478.6 4.2 convolution_convert_fusion.4
  482.8 0.9 copy-done.6
  483.7 3.9 fusion.82
  487.6 12.9 fusion.52
  500.5 13.3 bitcast_convert_fusion.1
  513.8 8.3 bitcast_convert_fusion
  522.2 13.9 convolution_convert_fusion.2
  536.2 122.2 %reduce-scatter.11.cloned.1.call-done = bf16[1600,1600]{1,0:T(8,128)(2,1)} async-done(((bf16[6400,1600]{1,0:T(8,128)(2,1)}), bf16[1600,1600]{1,0:T(8,128)(2,1)}) %reduce-scatter.11.cloned.1.call-update) | async-done | bytes 5120016 | tf_op jit(solution)/shard_map/reduce_scatter | solution.py:335
  658.4 158.1 %reduce-scatter.9.cloned.1.call-done = bf16[400,6400]{1,0:T(8,128)(2,1)} async-done(((bf16[1600,6400]{1,0:T(8,128)(2,1)}), bf16[400,6400]{1,0:T(8,128)(2,1)}) %reduce-scatter.9.cloned.1.call-update) | async-done | bytes 5120016 | tf_op jit(solution)/shard_map/reduce_scatter | solution.py:329
  816.6 122.5 %reduce-scatter.5.cloned.1.call-done = bf16[400,4800]{1,0:T(8,128)(2,1)} async-done(((bf16[1600,4800]{1,0:T(8,128)(2,1)}), bf16[400,4800]{1,0:T(8,128)(2,1)}) %reduce-scatter.5.cloned.1.call-update) | async-done | bytes 3840016 | tf_op jit(solution)/shard_map/reduce_scatter | solution.py:308
  940.4 0.3 dynamic-update-slice.8
  940.7 1.7 bitcast_reduce_fusion
  942.5 1.7 bitcast_reduce_fusion.1
  944.3 13.5 fusion.44
  957.8 11.5 all-reduce.20
  970.0 39.5 %all-reduce.18 = (bf16[400]{0:T(512)(128)(2,1)S(1)}, bf16[400]{0:T(512)(128)(2,1)S(1)}, bf16[400]{0:T(512)(128)(2,1)S(1)}, bf16[400]{0:T(512)(128)(2,1)S(1)}, bf...) all-reduce(bf16[400]{0:T(512)(128)(2,1)S(1)} %dynamic-slice.10, ...), channel_id=1, replica_groups=mesh['shard'=4,'replica'=8] {'replica'}, use_global_device_ids=true, to_apply=%region_15.16 | all-reduce | flops 4800 | bytes 19200 | tf_op jit(solution)/shard_map/psum | solution.py:343
  1009.5 0.6 convert_element_type.224
  1010.1 0.6 convert_element_type.226
  1010.6 0.6 convert_element_type.231
  1011.2 0.6 convert_element_type.234
  1011.8 0.6 convert_element_type.238
  1012.4 0.6 convert_element_type.240
  1013.0 0.6 convert_element_type.242
  1013.5 0.6 convert_element_type.250
  1014.1 0.6 convert_element_type.246
  1014.7 3.1 fusion.43
  1017.8 17.6 fusion.30
  1035.4 270.6 %all-reduce.24.cloned.1.call-done = (bf16[400,1600]{1,0:T(8,128)(2,1)}, bf16[400,6400]{1,0:T(8,128)(2,1)}, bf16[1600,1600]{1,0:T(8,128)(2,1)}) async-done(((bf16[400,1600]{1,0:T(8,128)(2,1)}, bf16[400,6400]{1,0:T(8,128)(2,1)}, bf16[1600,1600]{1,0:T(8,128)(2,1)}), (bf16[400,1600]{1,0:T(8,128)(2,1)}, bf16[400,6400]{1,0:T(8,128)(2,1)}, bf16[1600,1600]{1,0:T(8,128)(2,1)})) %all-reduce.24.cloned.1.call-update) | async-done | bytes 11520016 | tf_op jit(solution)/shard_map/psum | solution.py:350
  1306.0 3.1 convert_element_type.236
  1309.2 7.7 convert_element_type.244
  1316.9 4.8 convert_element_type.248
  1321.7 576.9 %all-gather.15.cloned.1.call-done = bf16[3200,4800]{1,0:T(8,128)(2,1)} async-done(((bf16[400,4800]{1,0:T(8,128)(2,1)}), bf16[3200,4800]{1,0:T(8,128)(2,1)}) %all-gather.15.cloned.1.call-update) | async-done | bytes 30720016 | tf_op jit(solution)/shard_map/all_gather | solution.py:345
  1898.6 13.4 reduce_sum.205
  1912.0 5.8 convert_element_type.228
  (116 shorter events, 3.8 us)
Async XLA Ops:
  7.2 104.3 %all-gather.7.cloned.1.call-start = ((), (), s32[]{:S(2)}) async-start(), calls=%async_computation.4 | async-start | bytes 19456000 | tf_op jit(solution)/shard_map/all_gather | solution.py:270
  7.9 146.1 %all-gather.9.cloned.1.call-start = ((), (), s32[]{:S(2)}) async-start(), calls=%async_computation.5 | async-start | bytes 6656000 | tf_op jit(solution)/shard_map/all_gather | solution.py:273
  8.7 1.5 copy-start.12
  8.7 3.4 copy-start.14
  8.7 3.7 copy-start.15
  8.7 3.9 copy-start.16
  8.7 4.1 copy-start.17
  8.7 4.4 copy-start.18
  8.7 4.6 copy-start.19
  8.7 4.9 copy-start.20
  8.8 5.1 copy-start.11
  8.8 19.7 %copy-start.13 = (s32[128]{0:T(128)S(1)}, s32[128]{0:T(128)}, u32[]{:S(2)}) copy-start(s32[128]{0:T(128)} %param.35) | copy-start | bytes 1540
  8.8 19.7 %copy-start.22 = (s32[128]{0:T(128)S(1)}, s32[128]{0:T(128)}, u32[]{:S(2)}) copy-start(s32[128]{0:T(128)} %param.33) | copy-start | bytes 1540
  8.8 19.8 %copy-start.23 = (s32[128]{0:T(128)S(1)}, s32[128]{0:T(128)}, u32[]{:S(2)}) copy-start(s32[128]{0:T(128)} %param.34) | copy-start | bytes 1540
  8.8 20.1 %copy-start.1 = (bf16[256,1600]{0,1:T(8,128)(2,1)S(1)}, bf16[256,1600]{0,1:T(8,128)(2,1)}, u32[]{:S(2)}) copy-start(bf16[256,1600]{0,1:T(8,128)(2,1)} %param.18) | copy-start | bytes 2457604
  8.8 275.7 %all-gather.11.cloned.1.call-start = ((), (), s32[]{:S(2)}) async-start(), calls=%async_computation.6 | async-start | bytes 25600000 | tf_op jit(solution)/shard_map/all_gather | solution.py:277
  9.5 409.8 %all-gather.13.cloned.1.call-start = ((), (), s32[]{:S(2)}) async-start(), calls=%async_computation.7 | async-start | bytes 26624000 | tf_op jit(solution)/shard_map/all_gather | solution.py:279
  10.1 526.1 %reduce-scatter.7.cloned.1.call-start = ((), (), s32[]{:S(2)}) async-start(), calls=%async_computation.9 | async-start | bytes 6656000 | tf_op jit(solution)/shard_map/reduce_scatter | solution.py:317
  127.5 0.9 copy-start.2
  127.5 2.2 copy-start.3
  127.5 3.3 copy-start.4
  129.7 2.8 copy-start
  134.2 24.7 %copy-start.7 = (bf16[25,64,256]{2,1,0:T(8,128)(2,1)}, bf16[25,64,256]{2,1,0:T(8,128)(2,1)S(1)}, u32[]{:S(2)}) copy-start(bf16[25,64,256]{2,1,0:T(8,128)(2,1)S(1)} %fusion.51) | copy-start | bytes 2457604
  159.2 260.2 %copy-start.9 = (bf16[256,1600]{0,1:T(8,128)(2,1)S(1)}, bf16[256,1600]{0,1:T(8,128)(2,1)}, u32[]{:S(2)}) copy-start(bf16[256,1600]{0,1:T(8,128)(2,1)} %param.32) | copy-start | bytes 2457604
  432.9 13.3 copy-start.10
  446.2 1.1 copy-start.8
  451.4 207.0 %reduce-scatter.11.cloned.1.call-start = ((), (), s32[]{:S(2)}) async-start(), calls=%async_computation.11 | async-start | bytes 26624000 | tf_op jit(solution)/shard_map/reduce_scatter | solution.py:335
  466.0 350.5 %reduce-scatter.9.cloned.1.call-start = ((), (), s32[]{:S(2)}) async-start(), calls=%async_computation.10 | async-start | bytes 25600000 | tf_op jit(solution)/shard_map/reduce_scatter | solution.py:329
  478.3 460.8 %reduce-scatter.5.cloned.1.call-start = ((), (), s32[]{:S(2)}) async-start(), calls=%async_computation.8 | async-start | bytes 19456000 | tf_op jit(solution)/shard_map/reduce_scatter | solution.py:308
  478.6 5.1 copy-start.5
  482.8 0.9 copy-start.6
  536.1 769.9 %all-reduce.24.cloned.1.call-start = ((), (), s32[]{:S(2)}) async-start(), calls=%async_computation.13 | async-start | bytes 23552000 | tf_op jit(solution)/shard_map/psum | solution.py:350
  816.5 123.9 %copy-start.21 = (bf16[400]{0:T(512)(128)(2,1)S(1)}, bf16[400]{0:T(512)(128)(2,1)}, u32[]{:S(2)}) copy-start(bf16[400]{0:T(512)(128)(2,1)} %param.31) | copy-start | bytes 2404
  816.6 1082.1 %all-gather.15.cloned.1.call-start = ((), (), s32[]{:S(2)}) async-start(), calls=%async_computation.12 | async-start | bytes 35020800 | tf_op jit(solution)/shard_map/all_gather | solution.py:345
  1306.0 10.8 slice-start
  1309.2 7.7 slice-start.1
Sparse Core Ops, SparseCore 0:
  9.5 101.8 all-gather.6
  113.0 40.9 all-gather.8
  155.6 128.8 all-gather.10
  285.9 133.3 all-gather.12
  451.5 51.8 reduce-scatter.6
  505.9 152.4 reduce-scatter.10
  661.0 155.4 reduce-scatter.8
  819.2 119.8 reduce-scatter.4
  943.5 362.5 all-reduce.23
  1307.4 591.1 all-gather.14
